TPU v7x, 32 devices: a whole 2x2x4 slice. The times are simulated.
32 devices in a mesh: dp: 4 (over y, x), expert: 8 (over z, core).
Axes of the slice: x: 2, y: 2, z: 4, core: 2. Of those that a mesh axis runs over, the one named last changes fastest.
Arguments:
- out_grad: bfloat16 [4096, 2048], P(('dp', 'expert')), may hold values from -1.1953125 to 1.1953125
- saved_hidden: bfloat16 [4096, 8, 384], P(('dp', 'expert')), may hold values from -6 to 6
- gate_weight: bfloat16 [4096, 8], P(('dp', 'expert')), may hold values from 0.19921875 to 1
- expert_ids: int32 [4096, 8], P(('dp', 'expert')), may hold values from 0 to 31, all different within a row; in each aligned block of 128 rows (0 to 127, 128 to 255, ...) at most 48 rows name the same one
- down_weight: bfloat16 [2048, 32, 384], P('dp', 'expert'), may hold values from -0.3125 to 0.3125
Outputs:
- grad_hidden: bfloat16 [4096, 8, 384], P(('dp', 'expert'))
- grad_gate: bfloat16 [4096, 8], P(('dp', 'expert'))
- grad_down: float32 [2048, 32, 384], P('dp', 'expert')
Inputs may be any that keep to these rules, and one draw needn't show every extreme that they name: `expert_ids`: each token names 8 different experts. Among the tokens of one device no expert is named by more than 48 tokens, and in every draw some expert is named by exactly 48 tokens of some device.
All inputs are finite; a program needn't handle non-finite values.
Results may differ from a plain program's by a relative error of at most 0.014.
Values may be sent and summed in bfloat16 or wider, within the bound.
A program may use at most 128 MiB of HBM per device.

v0:
```python
import jax
import jax.numpy as jnp
from jax import lax
from jax.sharding import PartitionSpec as P


def per_device(out_grad, saved_hidden, gate_weight, expert_ids, down_weight):
    tok_count = out_grad.shape[0]
    top_count = expert_ids.shape[1]
    width = out_grad.shape[1]
    hidden_width = saved_hidden.shape[2]
    owners = lax.axis_size("expert")
    local_experts = down_weight.shape[1]
    total_experts = local_experts * owners
    capacity = max(2, 3 * tok_count * top_count // (2 * total_experts))
    route_count = tok_count * top_count
    slot_count = total_experts * capacity
    flat_ids = expert_ids.reshape(route_count)
    one_hot = (flat_ids[:, None] == jnp.arange(total_experts, dtype=jnp.int32)[None, :]).astype(
        jnp.int32
    )
    before = jnp.cumsum(one_hot, axis=0) - one_hot
    position = jnp.sum(before * one_hot, axis=1)
    slot_of_route = flat_ids * capacity + position
    route_of_slot = (
        jnp.full((slot_count,), route_count, jnp.int32)
        .at[slot_of_route]
        .set(jnp.arange(route_count, dtype=jnp.int32))
    )
    token_of_slot = jnp.where(route_of_slot < route_count, route_of_slot // top_count, tok_count)
    grad_rows = jnp.concatenate([out_grad, jnp.zeros((1, width), out_grad.dtype)], axis=0)[
        token_of_slot
    ]
    hidden_rows = jnp.concatenate(
        [
            saved_hidden.reshape(route_count, hidden_width),
            jnp.zeros((1, hidden_width), saved_hidden.dtype),
        ],
        axis=0,
    )[route_of_slot]
    gate_rows = jnp.concatenate(
        [gate_weight.reshape(route_count), jnp.zeros((1,), gate_weight.dtype)], axis=0
    )[route_of_slot]
    grad_in, hidden_in, gate_in = (
        lax.all_to_all(grad_rows, "expert", split_axis=0, concat_axis=0, tiled=True),
        lax.all_to_all(hidden_rows, "expert", split_axis=0, concat_axis=0, tiled=True),
        lax.all_to_all(gate_rows, "expert", split_axis=0, concat_axis=0, tiled=True),
    )
    grid = (owners, local_experts, capacity)
    grad_in = grad_in.reshape(grid + (width,))
    hidden_in = hidden_in.reshape(grid + (hidden_width,))
    gate_in = gate_in.reshape(grid)
    scaled = (grad_in.astype(jnp.float32) * gate_in.astype(jnp.float32)[..., None]).astype(
        jnp.bfloat16
    )
    full_weight = lax.all_gather(down_weight, "dp", axis=0, tiled=True)
    scaled_part = scaled
    hidden_acc = jnp.einsum(
        "secd,def->secf", scaled_part, full_weight, preferred_element_type=jnp.float32
    )
    recomputed = jnp.einsum(
        "secf,def->secd", hidden_in, full_weight, preferred_element_type=jnp.float32
    )
    gate_acc = jnp.sum(grad_in.astype(jnp.float32) * recomputed, axis=3)
    scaled_part = scaled
    grad_down = lax.psum_scatter(
        jnp.einsum(
            "secd,secf->def", scaled_part, hidden_in, preferred_element_type=jnp.float32
        ).astype(jnp.bfloat16),
        "dp",
        scatter_dimension=0,
        tiled=True,
    ).astype(jnp.float32)
    back_hidden, back_gate = (
        lax.all_to_all(
            hidden_acc.astype(jnp.bfloat16).reshape(slot_count, hidden_width),
            "expert",
            split_axis=0,
            concat_axis=0,
            tiled=True,
        ),
        lax.all_to_all(
            gate_acc.astype(jnp.bfloat16).reshape(slot_count),
            "expert",
            split_axis=0,
            concat_axis=0,
            tiled=True,
        ),
    )
    grad_hidden = back_hidden[slot_of_route].reshape(tok_count, top_count, hidden_width)
    grad_gate = back_gate[slot_of_route].reshape(tok_count, top_count)
    return (grad_hidden, grad_gate, grad_down)


def solution(mesh):
    in_specs = (
        P(("dp", "expert"), None),
        P(("dp", "expert"), None, None),
        P(("dp", "expert"), None),
        P(("dp", "expert"), None),
        P("dp", "expert", None),
    )
    out_specs = (
        P(("dp", "expert"), None, None),
        P(("dp", "expert"), None),
        P("dp", "expert", None),
    )
    return jax.shard_map(
        per_device, mesh=mesh, in_specs=in_specs, out_specs=out_specs, check_vma=False
    )
```

profile of v0, /device:TPU:0, one launch (start us, length us, event | category | flops | bytes accessed | tf_op | source)
XLA Modules:
  0.0 313.0 jit_solution(17395364877933929451)
XLA Ops:
  7.2 0.9 copy.40
  8.9 9.0 %reduce-window.6 = s32[32,8,128]{2,1,0:T(8,128)S(1)} reduce-window(s32[32,8,128]{2,1,0:T(8,128)S(1)} %fusion.23, s32[]{:T(128)} %constant.17.clone.1), window={size=1x1x128 pad=0_0x0_0x127_0}, to_apply=%region_0.0 | reduce-window | flops 4161536 | bytes 262148 | tf_op jit(solution)/shard_map/reduce-window
  18.7 4.3 %scatter_custom_fusion = s32[1536]{0:T(1024)S(1)} fusion(s32[1024]{0:T(1024)S(1)} %bitcast.65, s32[1024]{0:T(1024)S(1)} %iota.11, s32[]{:T(128)} %constant.11.clone.1), kind=kCustom, calls=%fused_computation.42 | custom fusion | bytes 6148 | tf_op jit(solution)/shard_map/scatter | solution.py:28
  23.0 0.8 copy.44
  23.9 9.5 %gather_fusion.1 = bf16[1536]{0:T(1024)(128)(2,1)S(1)} fusion(bf16[1025]{0:T(1024)(128)(2,1)S(1)} %pad_maximum_fusion, s32[2048]{0:T(1024)S(1)} %get-tuple-element.17), kind=kCustom, calls=%fused_computation.1 | custom fusion | bytes 12288 | tf_op jit(solution)/shard_map/gather | solution.py:41
  34.1 6.4 %all-to-all-start.1 = ((bf16[8,192,1]{1,2,0:T(2,128)(2,1)}), bf16[8,192,1]{1,2,0:T(2,128)(2,1)S(1)}, u32[]{:S(2)}, u32[]{:S(2)}) async-start(bf16[8,192,1]{1,2,0:T(2,128)(2,1)} %all_to_all.43), calls=%async_computation.1 | async-start | bytes 16384 | tf_op jit(solution)/shard_map/all_to_all | solution.py:47
  40.6 5.3 %gather_fusion.3 = bf16[1536,384]{1,0:T(8,128)(2,1)} fusion(bf16[1025,384]{1,0:T(8,128)(2,1)S(1)} %concatenate.11, s32[2048]{0:T(1024)S(1)} %get-tuple-element.17), kind=kCustom, calls=%fused_computation.3 | custom fusion | bytes 2365440 | tf_op jit(solution)/shard_map/gather | solution.py:34
  46.1 4.9 %all-to-all-start.3 = ((bf16[8,192,384]{2,1,0:T(8,128)(2,1)}), bf16[8,192,384]{2,1,0:T(8,128)(2,1)S(1)}, u32[]{:S(2)}, u32[]{:S(2)}) async-start(bf16[8,192,384]{2,1,0:T(8,128)(2,1)} %bitcast.14), calls=%async_computation.3 | async-start | bytes 2359296 | tf_op jit(solution)/shard_map/all_to_all | solution.py:46
  51.0 7.1 %gather_fusion = bf16[1536,2048]{1,0:T(8,128)(2,1)} fusion(bf16[129,2048]{1,0:T(8,128)(2,1)S(1)} %concatenate.9, s32[2048]{0:T(1024)S(1)} %get-tuple-element.18), kind=kCustom, calls=%fused_computation | custom fusion | bytes 12589056 | tf_op jit(solution)/shard_map/gather | solution.py:31
  58.2 22.2 %all-to-all-done.3 = bf16[8,192,384]{2,1,0:T(8,128)(2,1)S(1)} async-done(((bf16[8,192,384]{2,1,0:T(8,128)(2,1)}), bf16[8,192,384]{2,1,0:T(8,128)(2,1)S(1)}, u32[]{:S(2)}, u32[]{:S(2)}) %all-to-all-start.3) | async-done | bytes 1179680 | tf_op jit(solution)/shard_map/all_to_all | solution.py:46
  80.3 4.9 %all-to-all-start = ((bf16[8,192,2048]{2,1,0:T(8,128)(2,1)}), bf16[8,192,2048]{2,1,0:T(8,128)(2,1)}, u32[]{:S(2)}, u32[]{:S(2)}) async-start(bf16[8,192,2048]{2,1,0:T(8,128)(2,1)} %bitcast.57), calls=%async_computation | async-start | bytes 12582912 | tf_op jit(solution)/shard_map/all_to_all | solution.py:45
  85.3 1.3 copy.46
  86.8 137.3 %all-to-all-done = bf16[8,192,2048]{2,1,0:T(8,128)(2,1)} async-done(((bf16[8,192,2048]{2,1,0:T(8,128)(2,1)}), bf16[8,192,2048]{2,1,0:T(8,128)(2,1)}, u32[]{:S(2)}, u32[]{:S(2)}) %all-to-all-start) | async-done | bytes 6291488 | tf_op jit(solution)/shard_map/all_to_all | solution.py:45
  224.1 9.0 %fusion.1 = bf16[2048,4,384]{0,2,1:T(8,128)(2,1)} fusion(bf16[8,4,48,384]{3,2,1,0:T(8,128)(2,1)S(1)} %bitcast.58, f32[8,4,48]{2,1,0:T(4,128)S(1)} %reshape.113, bf16[8,4,48,2048]{3,2,1,0:T(8,128)(2,1)} %bitcast.12), kind=kOutput, calls=%fused_computation.10 | convolution fusion | flops 2428502016 | bytes 13768704 | tf_op jit(solution)/shard_map/secd,secf->def/dot_general | solution.py:67
  233.2 8.7 %fusion = bf16[8,4,48]{2,0,1:T(8,128)(2,1)S(1)} fusion(bf16[2048,4,384]{2,0,1:T(8,128)(2,1)} %all-gather.2.cloned.1.call-done, bf16[8,4,48,384]{3,2,1,0:T(8,128)(2,1)S(1)} %bitcast.59, bf16[8,4,48,2048]{3,2,1,0:T(8,128)(2,1)} %bitcast.12), kind=kOutput, calls=%fused_computation.8 | convolution fusion | flops 2425354752 | bytes 13765632 | tf_op jit(solution)/shard_map/secf,def->secd/dot_general | solution.py:61
  242.6 3.5 %all-to-all-start.4 = ((bf16[8,192,1]{1,2,0:T(2,128)(2,1)}), bf16[8,192,1]{1,2,0:T(2,128)(2,1)S(1)}, u32[]{:S(2)}, u32[]{:S(2)}) async-start(bf16[8,192,1]{1,2,0:T(2,128)(2,1)} %convert_element_type.72), calls=%async_computation.4 | async-start | bytes 16384 | tf_op jit(solution)/shard_map/all_to_all | solution.py:82
  246.1 8.4 %fusion.14 = bf16[8,4,48,384]{3,2,0,1:T(8,128)(2,1)S(1)} fusion(bf16[2048,4,384]{2,0,1:T(8,128)(2,1)} %all-gather.2.cloned.1.call-done, f32[8,4,48]{2,1,0:T(4,128)S(1)} %reshape.113, bf16[8,4,48,2048]{3,2,1,0:T(8,128)(2,1)} %bitcast.12), kind=kOutput, calls=%fused_computation.17 | convolution fusion | flops 2425946112 | bytes 13768704 | tf_op jit(solution)/shard_map/secd,def->secf/dot_general | solution.py:58
  254.6 1.1 copy.48
  255.7 4.8 %all-to-all-start.2 = ((bf16[8,192,384]{2,1,0:T(8,128)(2,1)}), bf16[8,192,384]{2,1,0:T(8,128)(2,1)S(1)}, u32[]{:S(2)}, u32[]{:S(2)}) async-start(bf16[8,192,384]{2,1,0:T(8,128)(2,1)} %bitcast.9), calls=%async_computation.2 | async-start | bytes 2359296 | tf_op jit(solution)/shard_map/all_to_all | solution.py:75
  260.6 6.8 %gather_fusion.4 = bf16[1024]{0:T(1024)(128)(2,1)S(1)} fusion(bf16[1536]{0:T(1024)(128)(2,1)S(1)} %all_to_all.42, s32[1024]{0:T(1024)S(1)} %broadcast_clamp_fusion), kind=kCustom, calls=%fused_computation.4 | custom fusion | bytes 8192 | tf_op jit(solution)/shard_map/gather | solution.py:91
  268.2 21.7 %all-to-all-done.2 = bf16[8,192,384]{2,1,0:T(8,128)(2,1)S(1)} async-done(((bf16[8,192,384]{2,1,0:T(8,128)(2,1)}), bf16[8,192,384]{2,1,0:T(8,128)(2,1)S(1)}, u32[]{:S(2)}, u32[]{:S(2)}) %all-to-all-start.2) | async-done | bytes 1179680 | tf_op jit(solution)/shard_map/all_to_all | solution.py:75
  289.9 5.0 %gather_fusion.2 = bf16[1024,384]{1,0:T(8,128)(2,1)} fusion(bf16[1536,384]{1,0:T(8,128)(2,1)S(1)} %bitcast.56, s32[1024]{0:T(1024)S(1)} %broadcast_clamp_fusion), kind=kCustom, calls=%fused_computation.2 | custom fusion | bytes 1576960 | tf_op jit(solution)/shard_map/gather | solution.py:90
  294.9 7.4 %reduce-scatter.2.cloned.1.call-done = bf16[512,4,384]{0,2,1:T(8,128)(2,1)} async-done(((bf16[2048,4,384]{0,2,1:T(8,128)(2,1)}), bf16[512,4,384]{0,2,1:T(8,128)(2,1)}) %reduce-scatter.2.cloned.1.call-update) | async-done | bytes 1572880 | tf_op jit(solution)/shard_map/reduce_scatter | solution.py:66
  302.3 3.9 %copy.54 = f32[512,4,384]{2,1,0:T(4,128)} copy(bf16[512,4,384]{0,2,1:T(8,128)(2,1)} %reduce-scatter.2.cloned.1.call-done) | data formatting | bytes 4718592
  (44 shorter events, 4.5 us)
Async XLA Ops:
  7.2 33.3 %copy-start.1 = (bf16[128,8,384]{2,1,0:T(8,128)(2,1)S(1)}, bf16[128,8,384]{2,1,0:T(8,128)(2,1)}, u32[]{:S(2)}) copy-start(bf16[128,8,384]{2,1,0:T(8,128)(2,1)} %param.6) | copy-start | bytes 2359300
  34.1 12.0 %all-to-all-start.1 = ((bf16[8,192,1]{1,2,0:T(2,128)(2,1)}), bf16[8,192,1]{1,2,0:T(2,128)(2,1)S(1)}, u32[]{:S(2)}, u32[]{:S(2)}) async-start(bf16[8,192,1]{1,2,0:T(2,128)(2,1)} %all_to_all.43), calls=%async_computation.1 | async-start | bytes 16384 | tf_op jit(solution)/shard_map/all_to_all | solution.py:47
  40.5 10.4 %copy-start.2 = (bf16[128,2048]{1,0:T(8,128)(2,1)S(1)}, bf16[128,2048]{1,0:T(8,128)(2,1)}, u32[]{:S(2)}) copy-start(bf16[128,2048]{1,0:T(8,128)(2,1)} %param.5) | copy-start | bytes 1572868
  46.1 34.3 %all-to-all-start.3 = ((bf16[8,192,384]{2,1,0:T(8,128)(2,1)}), bf16[8,192,384]{2,1,0:T(8,128)(2,1)S(1)}, u32[]{:S(2)}, u32[]{:S(2)}) async-start(bf16[8,192,384]{2,1,0:T(8,128)(2,1)} %bitcast.14), calls=%async_computation.3 | async-start | bytes 2359296 | tf_op jit(solution)/shard_map/all_to_all | solution.py:46
  80.3 4.9 %copy-start = (bf16[512,4,384]{2,1,0:T(4,128)(2,1)S(1)}, bf16[512,4,384]{2,1,0:T(4,128)(2,1)}, u32[]{:S(2)}) copy-start(bf16[512,4,384]{2,1,0:T(4,128)(2,1)} %param.9) | copy-start | bytes 4718596
  80.3 143.8 %all-to-all-start = ((bf16[8,192,2048]{2,1,0:T(8,128)(2,1)}), bf16[8,192,2048]{2,1,0:T(8,128)(2,1)}, u32[]{:S(2)}, u32[]{:S(2)}) async-start(bf16[8,192,2048]{2,1,0:T(8,128)(2,1)} %bitcast.57), calls=%async_computation | async-start | bytes 12582912 | tf_op jit(solution)/shard_map/all_to_all | solution.py:45
  85.2 148.0 %all-gather.2.cloned.1.call-start = ((), (), s32[]{:S(2)}) async-start(), calls=%async_computation.6 | async-start | bytes 7864320 | tf_op jit(solution)/shard_map/all_gather | solution.py:56
  86.6 215.6 %reduce-scatter.2.cloned.1.call-start = ((), (), s32[]{:S(2)}) async-start(), calls=%async_computation.7 | async-start | bytes 7864320 | tf_op jit(solution)/shard_map/reduce_scatter | solution.py:66
  242.6 13.1 %all-to-all-start.4 = ((bf16[8,192,1]{1,2,0:T(2,128)(2,1)}), bf16[8,192,1]{1,2,0:T(2,128)(2,1)S(1)}, u32[]{:S(2)}, u32[]{:S(2)}) async-start(bf16[8,192,1]{1,2,0:T(2,128)(2,1)} %convert_element_type.72), calls=%async_computation.4 | async-start | bytes 16384 | tf_op jit(solution)/shard_map/all_to_all | solution.py:82
  255.7 34.1 %all-to-all-start.2 = ((bf16[8,192,384]{2,1,0:T(8,128)(2,1)}), bf16[8,192,384]{2,1,0:T(8,128)(2,1)S(1)}, u32[]{:S(2)}, u32[]{:S(2)}) async-start(bf16[8,192,384]{2,1,0:T(8,128)(2,1)} %bitcast.9), calls=%async_computation.2 | async-start | bytes 2359296 | tf_op jit(solution)/shard_map/all_to_all | solution.py:75
Sparse Core Ops, SparseCore 0:
  88.4 71.3 all-gather.1
  233.3 68.9 reduce-scatter.1
where the time goes:
time: 314 us; the launch traced here: 313 us
  waiting for transfers between devices  189 us (60%)
  local copies, waits for them, and re-layouts  49.3 us (16%)
  matrix products  26.2 us (8%)
  starting transfers between devices  24.5 us (8%)
  between operations  14.2 us (5%)
  other arithmetic  9.99 us (3%)
    all_to_all x1, waiting for transfers between devices, per_device(): lax.all_to_all(grad_rows, 'expert', split_axis=0, concat_axis=0, tiled=True)  137 us
    all_to_all x1, waiting for transfers between devices, per_device(): lax.all_to_all(hidden_rows, 'expert', split_axis=0, concat_axis=0, tiled=...  22.2 us
    all_to_all x1, waiting for transfers between devices, per_device(): lax.all_to_all(hidden_acc.astype(jnp.bfloat16).reshape(slot_count, hidden...  21.7 us
    gather x1, local copies, waits for them, and re-layouts, per_device(): jnp.concatenate([gate_weight.reshape(route_count), jnp.zeros((1,), gate_w...  9.46 us
    another operation x3, other arithmetic  9.15 us
    dot_general x1, matrix products, per_device(): jnp.einsum('secd,secf->def', scaled_part, hidden_in, preferred_element_ty...  9 us
    dot_general x1, matrix products, per_device(): jnp.einsum('secf,def->secd', hidden_in, full_weight, preferred_element_ty...  8.74 us
    dot_general x1, matrix products, per_device(): jnp.einsum('secd,def->secf', scaled_part, full_weight, preferred_element_...  8.41 us
  transfers between devices with their start and end apart: 7, of which 5 were waited for; matrix products, arithmetic and copies ran while one was open for 17% of the time, Pallas kernels for 0%

commit v1 on v0

--- a/solution.py
+++ b/solution.py
@@ -2,6 +2,29 @@
 import jax.numpy as jnp
 from jax import lax
 from jax.sharding import PartitionSpec as P
+
+
+def in_blocks(shard, dim, size):
+    before, after = (shard.shape[:dim], shard.shape[dim + 1 :])
+    return jnp.moveaxis(shard.reshape(*before, size, -1, *after), dim, 0)
+
+
+def in_order(pieces, dim):
+    shape = list(pieces.shape[1:])
+    shape[dim] *= pieces.shape[0]
+    return jnp.moveaxis(pieces, 0, dim).reshape(shape)
+
+
+def sent_to_each(array, axis, split_dim, concat_dim):
+    peers, index = (lax.axis_size(axis), lax.axis_index(axis))
+    tiles = in_blocks(array, split_dim, peers)
+    out = tiles
+    for lap in range(1, peers):
+        target, source = ((index + lap) % peers, (index - lap) % peers)
+        sent = lax.dynamic_index_in_dim(tiles, target, 0)
+        other = lax.ppermute(sent, axis, [(i, (i + lap) % peers) for i in range(peers)])
+        out = lax.dynamic_update_slice_in_dim(out, other, source, axis=0)
+    return in_order(out, concat_dim)
 
 
 def per_device(out_grad, saved_hidden, gate_weight, expert_ids, down_weight):
@@ -72,12 +95,8 @@
         tiled=True,
     ).astype(jnp.float32)
     back_hidden, back_gate = (
-        lax.all_to_all(
-            hidden_acc.astype(jnp.bfloat16).reshape(slot_count, hidden_width),
-            "expert",
-            split_axis=0,
-            concat_axis=0,
-            tiled=True,
+        sent_to_each(
+            hidden_acc.astype(jnp.bfloat16).reshape(slot_count, hidden_width), "expert", 0, 0
         ),
         lax.all_to_all(
             gate_acc.astype(jnp.bfloat16).reshape(slot_count),

time: 314 us -> 314 us (level)
  starting transfers between devices: 24.5 us -> 28.4 us
  matrix products: 26.2 us -> 23 us
    all_to_all x1 -> x0, waiting for transfers between devices: 21.7 us -> none  [per_device(): lax.all_to_all(hidden_acc.astype(jnp.bfloat16).reshape(slot_count, hidden...]
    reduce_scatter x1, waiting for transfers between devices: 7.39 us -> 18.7 us  [per_device(): lax.psum_scatter(jnp.einsum('secd,secf->def', scaled_part, hidden_in, pre...]
    ppermute x0 -> x7, waiting for transfers between devices: none -> 7.65 us  [sent_to_each(): lax.ppermute(sent, axis, [(i, (i + lap) % peers) for i in range(peers)])]
    ppermute x0 -> x7, starting transfers between devices: none -> 7.31 us  [sent_to_each(): lax.ppermute(sent, axis, [(i, (i + lap) % peers) for i in range(peers)])]
    all_to_all x1 -> x0, starting transfers between devices: 4.78 us -> none  [per_device(): lax.all_to_all(hidden_acc.astype(jnp.bfloat16).reshape(slot_count, hidden...]
    unnamed x11 -> x13, local copies, waits for them, and re-layouts: 7.57 us -> 7.5 us
  transfers between devices with their start and end apart: 7 -> 13, of which waited for: 5 -> 8; matrix products, arithmetic and copies ran while one was open for 17% -> 16% of each run, Pallas kernels for 0% -> 0%
where the time goes in v1:
time: 314 us; the launch traced here: 313 us
  waiting for transfers between devices  189 us (60%)
  local copies, waits for them, and re-layouts  48.5 us (15%)
  starting transfers between devices  28.4 us (9%)
  matrix products  23 us (7%)
  between operations  14.4 us (5%)
  other arithmetic  9.99 us (3%)
    all_to_all x1, waiting for transfers between devices, per_device(): lax.all_to_all(grad_rows, 'expert', split_axis=0, concat_axis=0, tiled=True)  137 us
    all_to_all x1, waiting for transfers between devices, per_device(): lax.all_to_all(hidden_rows, 'expert', split_axis=0, concat_axis=0, tiled=...  22.2 us
    reduce_scatter x1, waiting for transfers between devices, per_device(): lax.psum_scatter(jnp.einsum('secd,secf->def', scaled_part, hidden_in, pre...  18.7 us
    gather x1, local copies, waits for them, and re-layouts, per_device(): jnp.concatenate([gate_weight.reshape(route_count), jnp.zeros((1,), gate_w...  9.46 us
    another operation x3, other arithmetic  9.15 us
    dot_general x1, matrix products, per_device(): jnp.einsum('secd,secf->def', scaled_part, hidden_in, preferred_element_ty...  8.98 us
    dot_general x1, matrix products, per_device(): jnp.einsum('secd,def->secf', scaled_part, full_weight, preferred_element_...  8.2 us
    ppermute x7, waiting for transfers between devices, sent_to_each(): lax.ppermute(sent, axis, [(i, (i + lap) % peers) for i in range(peers)])  7.65 us
  transfers between devices with their start and end apart: 13, of which 8 were waited for; matrix products, arithmetic and copies ran while one was open for 16% of the time, Pallas kernels for 0%

profile of v1, /device:TPU:0, one launch (start us, length us, event | category | flops | bytes accessed | tf_op | source)
XLA Modules:
  0.0 313.0 jit_solution(4674375953453696558)
XLA Ops:
  10.0 9.0 %reduce-window.6 = s32[32,8,128]{2,1,0:T(8,128)S(1)} reduce-window(s32[32,8,128]{2,1,0:T(8,128)S(1)} %fusion.23, s32[]{:T(128)} %constant.125.clone.1), window={size=1x1x128 pad=0_0x0_0x127_0}, to_apply=%region_0.0 | reduce-window | flops 4161536 | bytes 262148 | tf_op jit(solution)/shard_map/reduce-window
  19.5 4.3 %scatter_custom_fusion = s32[1536]{0:T(1024)S(1)} fusion(s32[1024]{0:T(1024)S(1)} %bitcast.67, s32[1024]{0:T(1024)S(1)} %iota.11, s32[]{:T(128)} %constant.123.clone.1), kind=kCustom, calls=%fused_computation.42 | custom fusion | bytes 6148 | tf_op jit(solution)/shard_map/scatter | solution.py:51
  23.9 9.5 %gather_fusion.1 = bf16[1536]{0:T(1024)(128)(2,1)S(1)} fusion(bf16[1025]{0:T(1024)(128)(2,1)S(1)} %pad_maximum_fusion, s32[2048]{0:T(1024)S(1)} %get-tuple-element.24), kind=kCustom, calls=%fused_computation.1 | custom fusion | bytes 12288 | tf_op jit(solution)/shard_map/gather | solution.py:64
  34.0 6.4 %all-to-all-start.1 = ((bf16[8,192,1]{1,2,0:T(2,128)(2,1)}), bf16[8,192,1]{1,2,0:T(2,128)(2,1)S(1)}, u32[]{:S(2)}, u32[]{:S(2)}) async-start(bf16[8,192,1]{1,2,0:T(2,128)(2,1)} %all_to_all.32), calls=%async_computation.1 | async-start | bytes 16384 | tf_op jit(solution)/shard_map/all_to_all | solution.py:70
  40.5 5.3 %gather_fusion.3 = bf16[1536,384]{1,0:T(8,128)(2,1)} fusion(bf16[1025,384]{1,0:T(8,128)(2,1)S(1)} %concatenate.11, s32[2048]{0:T(1024)S(1)} %get-tuple-element.24), kind=kCustom, calls=%fused_computation.3 | custom fusion | bytes 2365440 | tf_op jit(solution)/shard_map/gather | solution.py:57
  46.0 5.0 %all-to-all-start.2 = ((bf16[8,192,384]{2,1,0:T(8,128)(2,1)}), bf16[8,192,384]{2,1,0:T(8,128)(2,1)S(1)}, u32[]{:S(2)}, u32[]{:S(2)}) async-start(bf16[8,192,384]{2,1,0:T(8,128)(2,1)} %bitcast.14), calls=%async_computation.2 | async-start | bytes 2359296 | tf_op jit(solution)/shard_map/all_to_all | solution.py:69
  51.1 7.1 %gather_fusion = bf16[1536,2048]{1,0:T(8,128)(2,1)} fusion(bf16[129,2048]{1,0:T(8,128)(2,1)S(1)} %concatenate.9, s32[2048]{0:T(1024)S(1)} %get-tuple-element.25), kind=kCustom, calls=%fused_computation | custom fusion | bytes 12589056 | tf_op jit(solution)/shard_map/gather | solution.py:54
  58.2 22.2 %all-to-all-done.2 = bf16[8,192,384]{2,1,0:T(8,128)(2,1)S(1)} async-done(((bf16[8,192,384]{2,1,0:T(8,128)(2,1)}), bf16[8,192,384]{2,1,0:T(8,128)(2,1)S(1)}, u32[]{:S(2)}, u32[]{:S(2)}) %all-to-all-start.2) | async-done | bytes 1179680 | tf_op jit(solution)/shard_map/all_to_all | solution.py:69
  80.4 4.9 %all-to-all-start = ((bf16[8,192,2048]{2,1,0:T(8,128)(2,1)}), bf16[8,192,2048]{2,1,0:T(8,128)(2,1)}, u32[]{:S(2)}, u32[]{:S(2)}) async-start(bf16[8,192,2048]{2,1,0:T(8,128)(2,1)} %bitcast.59), calls=%async_computation | async-start | bytes 12582912 | tf_op jit(solution)/shard_map/all_to_all | solution.py:68
  85.3 1.3 copy.46
  86.9 137.3 %all-to-all-done = bf16[8,192,2048]{2,1,0:T(8,128)(2,1)} async-done(((bf16[8,192,2048]{2,1,0:T(8,128)(2,1)}), bf16[8,192,2048]{2,1,0:T(8,128)(2,1)}, u32[]{:S(2)}, u32[]{:S(2)}) %all-to-all-start) | async-done | bytes 6291488 | tf_op jit(solution)/shard_map/all_to_all | solution.py:68
  224.2 9.0 %fusion.1 = bf16[2048,4,384]{0,2,1:T(8,128)(2,1)} fusion(bf16[8,4,48,384]{3,2,1,0:T(8,128)(2,1)S(1)} %bitcast.60, f32[8,4,48]{2,1,0:T(4,128)S(1)} %reshape.113, bf16[8,4,48,2048]{3,2,1,0:T(8,128)(2,1)} %bitcast.12), kind=kOutput, calls=%fused_computation.10 | convolution fusion | flops 2428502016 | bytes 13768704 | tf_op jit(solution)/shard_map/secd,secf->def/dot_general | solution.py:90
  233.3 8.2 %fusion.14 = bf16[8,4,48,384]{3,2,0,1:T(8,128)(2,1)S(1)} fusion(bf16[2048,4,384]{2,0,1:T(8,128)(2,1)} %all-gather.2.cloned.1.call-done, f32[8,4,48]{2,1,0:T(4,128)S(1)} %reshape.113, bf16[8,4,48,2048]{3,2,1,0:T(8,128)(2,1)} %bitcast.12), kind=kOutput, calls=%fused_computation.17 | convolution fusion | flops 2425946112 | bytes 13768704 | tf_op jit(solution)/shard_map/secd,def->secf/dot_general | solution.py:81
  242.0 5.8 %fusion = bf16[8,4,48]{2,0,1:T(8,128)(2,1)S(1)} fusion(bf16[2048,4,384]{2,0,1:T(8,128)(2,1)S(1)} %copy-done.3, bf16[8,4,48,384]{3,2,1,0:T(8,128)(2,1)S(1)} %bitcast.61, bf16[8,4,48,2048]{3,2,1,0:T(8,128)(2,1)} %bitcast.12), kind=kOutput, calls=%fused_computation.8 | convolution fusion | flops 2425354752 | bytes 13765632 | tf_op jit(solution)/shard_map/secf,def->secd/dot_general | solution.py:84
  248.5 4.8 %all-to-all-start.3 = ((bf16[8,192,1]{1,2,0:T(2,128)(2,1)}), bf16[8,192,1]{1,2,0:T(2,128)(2,1)S(1)}, u32[]{:S(2)}, u32[]{:S(2)}) async-start(bf16[8,192,1]{1,2,0:T(2,128)(2,1)} %convert_element_type.72), calls=%async_computation.3 | async-start | bytes 16384 | tf_op jit(solution)/shard_map/all_to_all | solution.py:101
  253.5 2.1 collective-permute-start.1
  256.4 2.5 all-to-all-done.3
  259.1 6.8 %gather_fusion.4 = bf16[1024]{0:T(1024)(128)(2,1)S(1)} fusion(bf16[1536]{0:T(1024)(128)(2,1)S(1)} %all_to_all.31, s32[1024]{0:T(1024)S(1)} %broadcast_clamp_fusion), kind=kCustom, calls=%fused_computation.4 | custom fusion | bytes 8192 | tf_op jit(solution)/shard_map/gather | solution.py:110
  267.2 1.5 collective-permute-start.4
  269.6 1.1 collective-permute-start.6
  270.8 7.2 %collective-permute-done.3 = bf16[1,192,384]{2,1,0:T(8,128)(2,1)S(1)} collective-permute-done((bf16[1,192,384]{2,1,0:T(8,128)(2,1)S(1)}, bf16[1,192,384]{2,1,0:T(8,128)(2,1)S(1)}, u32[]{:S(2)}, u32[]{:S(2)}) %collective-permute-start.3) | collective-permute-done | bytes 147488 | tf_op jit(solution)/shard_map/ppermute | solution.py:25
  278.6 5.0 %gather_fusion.2 = bf16[1024,384]{1,0:T(8,128)(2,1)} fusion(bf16[1536,384]{1,0:T(8,128)(2,1)S(1)} %bitcast.58, s32[1024]{0:T(1024)S(1)} %broadcast_clamp_fusion), kind=kCustom, calls=%fused_computation.2 | custom fusion | bytes 1576960 | tf_op jit(solution)/shard_map/gather | solution.py:109
  283.6 18.7 %reduce-scatter.2.cloned.1.call-done = bf16[512,4,384]{0,2,1:T(8,128)(2,1)} async-done(((bf16[2048,4,384]{0,2,1:T(8,128)(2,1)}), bf16[512,4,384]{0,2,1:T(8,128)(2,1)}) %reduce-scatter.2.cloned.1.call-update) | async-done | bytes 1572880 | tf_op jit(solution)/shard_map/reduce_scatter | solution.py:89
  302.3 3.9 %copy.54 = f32[512,4,384]{2,1,0:T(4,128)} copy(bf16[512,4,384]{0,2,1:T(8,128)(2,1)} %reduce-scatter.2.cloned.1.call-done) | data formatting | bytes 4718592
  (66 shorter events, 9.7 us)
Async XLA Ops:
  19.3 21.1 %copy-start.1 = (bf16[128,8,384]{2,1,0:T(8,128)(2,1)S(1)}, bf16[128,8,384]{2,1,0:T(8,128)(2,1)}, u32[]{:S(2)}) copy-start(bf16[128,8,384]{2,1,0:T(8,128)(2,1)} %param.6) | copy-start | bytes 2359300
  34.0 12.0 %all-to-all-start.1 = ((bf16[8,192,1]{1,2,0:T(2,128)(2,1)}), bf16[8,192,1]{1,2,0:T(2,128)(2,1)S(1)}, u32[]{:S(2)}, u32[]{:S(2)}) async-start(bf16[8,192,1]{1,2,0:T(2,128)(2,1)} %all_to_all.32), calls=%async_computation.1 | async-start | bytes 16384 | tf_op jit(solution)/shard_map/all_to_all | solution.py:70
  45.8 5.2 %copy-start.2 = (bf16[128,2048]{1,0:T(8,128)(2,1)S(1)}, bf16[128,2048]{1,0:T(8,128)(2,1)}, u32[]{:S(2)}) copy-start(bf16[128,2048]{1,0:T(8,128)(2,1)} %param.5) | copy-start | bytes 1572868
  46.0 34.4 %all-to-all-start.2 = ((bf16[8,192,384]{2,1,0:T(8,128)(2,1)}), bf16[8,192,384]{2,1,0:T(8,128)(2,1)S(1)}, u32[]{:S(2)}, u32[]{:S(2)}) async-start(bf16[8,192,384]{2,1,0:T(8,128)(2,1)} %bitcast.14), calls=%async_computation.2 | async-start | bytes 2359296 | tf_op jit(solution)/shard_map/all_to_all | solution.py:69
  80.4 5.0 %copy-start = (bf16[512,4,384]{2,1,0:T(4,128)(2,1)S(1)}, bf16[512,4,384]{2,1,0:T(4,128)(2,1)}, u32[]{:S(2)}) copy-start(bf16[512,4,384]{2,1,0:T(4,128)(2,1)} %param.9) | copy-start | bytes 4718596
  80.4 143.8 %all-to-all-start = ((bf16[8,192,2048]{2,1,0:T(8,128)(2,1)}), bf16[8,192,2048]{2,1,0:T(8,128)(2,1)}, u32[]{:S(2)}, u32[]{:S(2)}) async-start(bf16[8,192,2048]{2,1,0:T(8,128)(2,1)} %bitcast.59), calls=%async_computation | async-start | bytes 12582912 | tf_op jit(solution)/shard_map/all_to_all | solution.py:68
  85.3 148.1 %all-gather.2.cloned.1.call-start = ((), (), s32[]{:S(2)}) async-start(), calls=%async_computation.5 | async-start | bytes 7864320 | tf_op jit(solution)/shard_map/all_gather | solution.py:79
  86.7 215.6 %reduce-scatter.2.cloned.1.call-start = ((), (), s32[]{:S(2)}) async-start(), calls=%async_computation.6 | async-start | bytes 7864320 | tf_op jit(solution)/shard_map/reduce_scatter | solution.py:89
  233.3 8.6 %copy-start.3 = (bf16[2048,4,384]{2,0,1:T(8,128)(2,1)S(1)}, bf16[2048,4,384]{2,0,1:T(8,128)(2,1)}, u32[]{:S(2)}) copy-start(bf16[2048,4,384]{2,0,1:T(8,128)(2,1)} %all-gather.2.cloned.1.call-done) | copy-start | bytes 18874372
  241.7 11.6 %collective-permute-start = (bf16[1,192,384]{2,1,0:T(8,128)(2,1)S(1)}, bf16[1,192,384]{2,1,0:T(8,128)(2,1)S(1)}, u32[]{:S(2)}, u32[]{:S(2)}) collective-permute-start(bf16[1,192,384]{2,1,0:T(8,128)(2,1)S(1)} %constant_dynamic-slice_fusion.6), channel_id=1, source_target_pairs={{0,1},{1,2},{2,3},{3,4},{4,5},{5,6},{6,7},{7,0},{8,9},{9,10},{10,1... | collective-permute-start | bytes 442376 | tf_op jit(solution)/shard_map/ppermute | solution.py:25
  248.5 10.4 %all-to-all-start.3 = ((bf16[8,192,1]{1,2,0:T(2,128)(2,1)}), bf16[8,192,1]{1,2,0:T(2,128)(2,1)S(1)}, u32[]{:S(2)}, u32[]{:S(2)}) async-start(bf16[8,192,1]{1,2,0:T(2,128)(2,1)} %convert_element_type.72), calls=%async_computation.3 | async-start | bytes 16384 | tf_op jit(solution)/shard_map/all_to_all | solution.py:101
  253.5 16.2 %collective-permute-start.1 = (bf16[1,192,384]{2,1,0:T(8,128)(2,1)S(1)}, bf16[1,192,384]{2,1,0:T(8,128)(2,1)S(1)}, u32[]{:S(2)}, u32[]{:S(2)}) collective-permute-start(bf16[1,192,384]{2,1,0:T(8,128)(2,1)S(1)} %get-tuple-element.20), channel_id=1, source_target_pairs={{0,2},{1,3},{2,4},{3,5},{4,6},{5,7},{6,0},{7,1},{8,10},{9,11},{10,... | collective-permute-start | bytes 442376 | tf_op jit(solution)/shard_map/ppermute | solution.py:25
  255.5 15.3 %collective-permute-start.2 = (bf16[1,192,384]{2,1,0:T(8,128)(2,1)S(1)}, bf16[1,192,384]{2,1,0:T(8,128)(2,1)S(1)}, u32[]{:S(2)}, u32[]{:S(2)}) collective-permute-start(bf16[1,192,384]{2,1,0:T(8,128)(2,1)S(1)} %get-tuple-element.19), channel_id=1, source_target_pairs={{0,3},{1,4},{2,5},{3,6},{4,7},{5,0},{6,1},{7,2},{8,11},{9,12},{10,... | collective-permute-start | bytes 442376 | tf_op jit(solution)/shard_map/ppermute | solution.py:25
  266.7 11.4 %collective-permute-start.3 = (bf16[1,192,384]{2,1,0:T(8,128)(2,1)S(1)}, bf16[1,192,384]{2,1,0:T(8,128)(2,1)S(1)}, u32[]{:S(2)}, u32[]{:S(2)}) collective-permute-start(bf16[1,192,384]{2,1,0:T(8,128)(2,1)S(1)} %get-tuple-element.18), channel_id=1, source_target_pairs={{0,4},{1,5},{2,6},{3,7},{4,0},{5,1},{6,2},{7,3},{8,12},{9,13},{10,... | collective-permute-start | bytes 442376 | tf_op jit(solution)/shard_map/ppermute | solution.py:25
  267.2 10.9 %collective-permute-start.4 = (bf16[1,192,384]{2,1,0:T(8,128)(2,1)S(1)}, bf16[1,192,384]{2,1,0:T(8,128)(2,1)S(1)}, u32[]{:S(2)}, u32[]{:S(2)}) collective-permute-start(bf16[1,192,384]{2,1,0:T(8,128)(2,1)S(1)} %get-tuple-element.17), channel_id=1, source_target_pairs={{0,5},{1,6},{2,7},{3,0},{4,1},{5,2},{6,3},{7,4},{8,13},{9,14},{10,... | collective-permute-start | bytes 442376 | tf_op jit(solution)/shard_map/ppermute | solution.py:25
  268.7 9.8 %collective-permute-start.5 = (bf16[1,192,384]{2,1,0:T(8,128)(2,1)S(1)}, bf16[1,192,384]{2,1,0:T(8,128)(2,1)S(1)}, u32[]{:S(2)}, u32[]{:S(2)}) collective-permute-start(bf16[1,192,384]{2,1,0:T(8,128)(2,1)S(1)} %get-tuple-element.16), channel_id=1, source_target_pairs={{0,6},{1,7},{2,0},{3,1},{4,2},{5,3},{6,4},{7,5},{8,14},{9,15},{10,... | collective-permute-start | bytes 442376 | tf_op jit(solution)/shard_map/ppermute | solution.py:25
  269.6 9.0 %collective-permute-start.6 = (bf16[1,192,384]{2,1,0:T(8,128)(2,1)S(1)}, bf16[1,192,384]{2,1,0:T(8,128)(2,1)S(1)}, u32[]{:S(2)}, u32[]{:S(2)}) collective-permute-start(bf16[1,192,384]{2,1,0:T(8,128)(2,1)S(1)} %get-tuple-element.15), channel_id=1, source_target_pairs={{0,7},{1,0},{2,1},{3,2},{4,3},{5,4},{6,5},{7,6},{8,15},{9,8},{10,9... | collective-permute-start | bytes 442376 | tf_op jit(solution)/shard_map/ppermute | solution.py:25
Sparse Core Ops, SparseCore 0:
  88.5 71.3 all-gather.1
  233.3 68.9 reduce-scatter.1
